TPU v7x, 32 devices: a whole 2x2x4 slice. The times are simulated.
32 devices in a mesh: grp: 2 (over y), ctx: 4 (over z), head: 2 (over x), rep: 2 (over core).
Axes of the slice: x: 2, y: 2, z: 4, core: 2. Of those that a mesh axis runs over, the one named last changes fastest.
Arguments:
- queries: bfloat16 [8192, 2048], P(('grp', 'ctx', 'head', 'rep')), parts along dimension 0, may hold values from -10 to 10
- keys: bfloat16 [8192, 2048], P(('grp', 'ctx', 'head', 'rep')), parts along dimension 0, may hold values from -10 to 10
- values: bfloat16 [8192, 2048], P(('grp', 'ctx', 'head', 'rep')), parts along dimension 0, may hold values from -6 to 6
- reads: int32 [16, 8], P('grp'), parts along dimension 0, may hold values from 0 to 1, as said below
- owner: int32 [16], P('grp'), parts along dimension 0, may hold values from 0 to 7, as said below
Outputs:
- attended: bfloat16 [8192, 2048], P(('grp', 'ctx', 'head', 'rep')), parts along dimension 0
There are 2 independent parts, one for each index of `grp`. A program takes and returns all parts, laid end to end along the dimension named above; each array names one. Nothing has to cross between parts.
Inputs may be any that keep to these rules, and one draw needn't show every extreme that they name: `owner`: A permutation of the blocks in which sequence block b sits in slot b or in slot b with its lowest bit flipped. Every block reads itself; reads[kb, qb] is nonzero only where |kb - qb| <= 2 and |owner[kb] - owner[qb]| <= 3.
All inputs are finite; a program needn't handle non-finite values.
Results may differ from a plain program's by a relative error of at most 0.0047.
Values may be sent and summed in bfloat16 or wider, within the bound.
No kernel may reach another device: no remote copies, remote signals or barrier semaphores. Data moves between devices by JAX's collectives and lax.ppermute only.
A program may use at most 64 MiB of HBM per device.

v0:
```python
import math
import jax
import jax.numpy as jnp
from jax import lax
from jax.sharding import PartitionSpec as P

HEAD_DIM = 64
BLOCK = 512
REACH = 3


def from_behind(x, axis, by):
    devices = lax.axis_size(axis)
    pairs = [(i, i + by) for i in range(devices) if 0 <= i + by < devices]
    return lax.ppermute(x, axis, pairs)


def shards(queries, keys, values, reads, owner):
    query_heads, key_heads, value_heads = (
        lax.all_to_all(queries, ("head", "rep"), split_axis=1, concat_axis=0, tiled=True),
        lax.all_to_all(keys, ("head", "rep"), split_axis=1, concat_axis=0, tiled=True),
        lax.all_to_all(values, ("head", "rep"), split_axis=1, concat_axis=0, tiled=True),
    )
    row_count, feat_width = query_heads.shape
    heads_dev = feat_width // HEAD_DIM
    blk_dev = row_count // BLOCK
    reach_devs = -(-REACH // blk_dev)
    pair_kv = jnp.stack([key_heads, value_heads])
    lower_list = []
    upper_list = []
    moving = pair_kv
    for hop_index in range(reach_devs):
        moving = from_behind(moving, "ctx", 1)
        lower_list.insert(0, moving)
    moving = pair_kv
    for hop_index in range(reach_devs):
        moving = from_behind(moving, "ctx", -1)
        upper_list.append(moving)
    pieces = lower_list + [pair_kv] + upper_list
    window = jnp.concatenate(pieces, axis=1)
    highest = lax.Precision.HIGHEST
    block_count = reads.shape[0]
    slots = jnp.arange(block_count, dtype=jnp.int32)
    placed = (owner[:, None] == slots[None, :]).astype(jnp.float32)
    slot_reads = jnp.dot(
        jnp.dot(placed.T, reads.astype(jnp.float32), precision=highest), placed, precision=highest
    )
    padded_reads = jnp.pad(slot_reads, ((REACH, REACH), (0, 0)))
    ctx_index = lax.axis_index("ctx")
    scale_factor = 1.0 / math.sqrt(HEAD_DIM)
    tile_rows = min(512, BLOCK)
    tile_count = row_count // tile_rows

    def attend_tile(tile_id):
        local_block = tile_id * tile_rows // BLOCK
        query_slot = ctx_index * blk_dev + local_block
        column = lax.dynamic_index_in_dim(padded_reads, query_slot, 1, keepdims=False)
        allowed = lax.dynamic_slice_in_dim(column, query_slot, 2 * REACH + 1)
        query_tile = lax.dynamic_slice_in_dim(query_heads, tile_id * tile_rows, tile_rows, 0)
        query_tile = query_tile.reshape(tile_rows, heads_dev, HEAD_DIM)

        def key_block(relative):
            start = (reach_devs * blk_dev + local_block + relative) * BLOCK
            picked = lax.dynamic_slice_in_dim(window, start, BLOCK, 1)
            return picked.reshape(2, BLOCK, heads_dev, HEAD_DIM)

        def block_scores(kv_block):
            return (
                jnp.einsum(
                    "qhd,khd->hqk", query_tile, kv_block[0], preferred_element_type=jnp.float32
                )
                * scale_factor
            )

        def add_weights(pair, scores, value_block, row_max):
            weights = jnp.exp(scores - row_max[:, :, None])
            row_total = pair[1] + jnp.sum(weights, axis=-1)
            rounded = weights.astype(jnp.bfloat16)
            accum_out = pair[0] + jnp.einsum(
                "hqk,khd->qhd", rounded, value_block, preferred_element_type=jnp.float32
            )
            return (accum_out, row_total)

        row_max = jnp.full((heads_dev, tile_rows), -jnp.inf, jnp.float32)
        for position in range(2 * REACH + 1):
            is_read = allowed[position] > 0.5
            kv_block = key_block(position - REACH)
            row_max = lax.cond(
                is_read,
                lambda current, chosen=kv_block: jnp.maximum(
                    current, jnp.max(block_scores(chosen), axis=-1)
                ),
                lambda current: current,
                row_max,
            )
        totals = (
            jnp.zeros((tile_rows, heads_dev, HEAD_DIM), jnp.float32),
            jnp.zeros((heads_dev, tile_rows), jnp.float32),
        )
        for position in range(2 * REACH + 1):
            is_read = allowed[position] > 0.5
            kv_block = key_block(position - REACH)
            totals = lax.cond(
                is_read,
                lambda pair, chosen=kv_block: add_weights(
                    pair, block_scores(chosen), chosen[1], row_max
                ),
                lambda pair: pair,
                totals,
            )
        result = totals[0] / jnp.transpose(totals[1])[:, :, None]
        return result.reshape(tile_rows, feat_width).astype(jnp.bfloat16)

    tiles_out = lax.map(attend_tile, jnp.arange(tile_count, dtype=jnp.int32))
    attended = tiles_out.reshape(row_count, feat_width)
    return lax.all_to_all(attended, ("head", "rep"), split_axis=0, concat_axis=1, tiled=True)


def solution(mesh):
    placed = (
        P(("grp", "ctx", "head", "rep"), None),
        P(("grp", "ctx", "head", "rep"), None),
        P(("grp", "ctx", "head", "rep"), None),
        P("grp", None),
        P("grp"),
    )
    return jax.shard_map(
        shards,
        mesh=mesh,
        in_specs=placed,
        out_specs=P(("grp", "ctx", "head", "rep"), None),
        check_vma=False,
    )
```

profile of v0, /device:TPU:20, one launch (start us, length us, event | category | flops | bytes accessed | tf_op | source)
XLA Modules:
  0.0 273.8 jit_solution(7795582679675282533)
XLA Ops:
  2.3 3.5 %all-to-all-start = ((bf16[256,4,512]{0,2,1:T(8,128)(2,1)}), bf16[256,4,512]{0,2,1:T(8,128)(2,1)S(1)}, u32[]{:S(2)}, u32[]{:S(2)}) async-start(bf16[256,4,512]{0,2,1:T(8,128)(2,1)} %bitcast.46), calls=%async_computation | async-start | bytes 2097152 | tf_op jit(solution)/shard_map/all_to_all | solution.py:21
  8.1 12.1 %all-to-all-done = bf16[256,4,512]{0,2,1:T(8,128)(2,1)S(1)} async-done(((bf16[256,4,512]{0,2,1:T(8,128)(2,1)}), bf16[256,4,512]{0,2,1:T(8,128)(2,1)S(1)}, u32[]{:S(2)}, u32[]{:S(2)}) %all-to-all-start) | async-done | bytes 1048608 | tf_op jit(solution)/shard_map/all_to_all | solution.py:21
  20.2 3.5 %all-to-all-start.1 = ((bf16[256,4,512]{0,2,1:T(8,128)(2,1)}), bf16[256,4,512]{0,2,1:T(8,128)(2,1)S(1)}, u32[]{:S(2)}, u32[]{:S(2)}) async-start(bf16[256,4,512]{0,2,1:T(8,128)(2,1)} %bitcast.49), calls=%async_computation.1 | async-start | bytes 2097152 | tf_op jit(solution)/shard_map/all_to_all | solution.py:22
  24.3 13.8 %all-to-all-done.1 = bf16[256,4,512]{0,2,1:T(8,128)(2,1)S(1)} async-done(((bf16[256,4,512]{0,2,1:T(8,128)(2,1)}), bf16[256,4,512]{0,2,1:T(8,128)(2,1)S(1)}, u32[]{:S(2)}, u32[]{:S(2)}) %all-to-all-start.1) | async-done | bytes 1048608 | tf_op jit(solution)/shard_map/all_to_all | solution.py:22
  38.9 3.5 %collective-permute-start = (bf16[2,1024,512]{2,1,0:T(8,128)(2,1)S(1)}, bf16[2,1024,512]{2,1,0:T(8,128)(2,1)}, u32[]{:S(2)}, u32[]{:S(2)}) collective-permute-start(bf16[2,1024,512]{2,1,0:T(8,128)(2,1)S(1)} %pad_maximum_fusion), channel_id=1, source_target_pairs={{0,4},{4,8},{8,12},{1,5},{5,9},{9,13},{2,6},{6,10},{10,14},{3,7},{... | collective-permute-start | bytes 6291464 | tf_op jit(solution)/shard_map/ppermute | solution.py:15
  44.7 43.2 %collective-permute-done = bf16[2,1024,512]{2,1,0:T(8,128)(2,1)} collective-permute-done((bf16[2,1024,512]{2,1,0:T(8,128)(2,1)S(1)}, bf16[2,1024,512]{2,1,0:T(8,128)(2,1)}, u32[]{:S(2)}, u32[]{:S(2)}) %collective-permute-start) | collective-permute-done | bytes 2097184 | tf_op jit(solution)/shard_map/ppermute | solution.py:15
  87.9 3.5 %collective-permute-start.1 = (bf16[2,1024,512]{2,1,0:T(8,128)(2,1)}, bf16[2,1024,512]{2,1,0:T(8,128)(2,1)}, u32[]{:S(2)}, u32[]{:S(2)}) collective-permute-start(bf16[2,1024,512]{2,1,0:T(8,128)(2,1)} %collective-permute-done), channel_id=1, source_target_pairs={{0,4},{4,8},{8,12},{1,5},{5,9},{9,13},{2,6},{6,10},{10,14},{3,7},{... | collective-permute-start | bytes 6291464 | tf_op jit(solution)/shard_map/ppermute | solution.py:15
  96.1 3.5 %all-to-all-start.2 = ((bf16[256,4,512]{0,2,1:T(8,128)(2,1)}), bf16[256,4,512]{0,2,1:T(8,128)(2,1)S(1)}, u32[]{:S(2)}, u32[]{:S(2)}) async-start(bf16[256,4,512]{0,2,1:T(8,128)(2,1)} %bitcast.222), calls=%async_computation.2 | async-start | bytes 2097152 | tf_op jit(solution)/shard_map/all_to_all | solution.py:20
  100.2 13.8 %all-to-all-done.2 = bf16[256,4,512]{0,2,1:T(8,128)(2,1)S(1)} async-done(((bf16[256,4,512]{0,2,1:T(8,128)(2,1)}), bf16[256,4,512]{0,2,1:T(8,128)(2,1)S(1)}, u32[]{:S(2)}, u32[]{:S(2)}) %all-to-all-start.2) | async-done | bytes 1048608 | tf_op jit(solution)/shard_map/all_to_all | solution.py:20
  115.3 21.0 %collective-permute-done.1 = bf16[2,1024,512]{2,1,0:T(8,128)(2,1)} collective-permute-done((bf16[2,1024,512]{2,1,0:T(8,128)(2,1)}, bf16[2,1024,512]{2,1,0:T(8,128)(2,1)}, u32[]{:S(2)}, u32[]{:S(2)}) %collective-permute-start.1) | collective-permute-done | bytes 2097184 | tf_op jit(solution)/shard_map/ppermute | solution.py:15
  150.1 13.8 %copy.66 = bf16[2,5120,512]{1,2,0:T(8,128)(2,1)} copy(bf16[2,5120,512]{2,1,0:T(8,128)(2,1)} %constant_dynamic-update-slice_fusion.1) | data formatting | bytes 20971520 | tf_op jit(solution)/shard_map/while | solution.py:114
  163.9 90.1 %while.13 = (s32[]{:T(128)}, bf16[2,512,512]{2,1,0:T(8,128)(2,1)}, s32[2]{0:T(128)S(1)}, s32[]{:T(128)}, f32[14,8]{0,1:T(8,128)S(1)}, /*index=5*/bf16[2,5120,512...) while((s32[]{:T(128)}, bf16[2,512,512]{2,1,0:T(8,128)(2,1)}, ...), condition=%wide.region_43.44_spmd, body=%wide.region_0.43_spmd.sunk | while | flops 5756674048 | bytes 200296880 | solution.py:114
  165.2 5.5 %constant_dynamic-slice_fusion.10 = (bf16[2,512,512]{1,2,0:T(8,128)(2,1)S(1)}, bf16[2,512,512]{1,2,0:T(8,128)(2,1)}, bf16[2,512,512]{1,2,0:T(8,128)(2,1)}, bf16[...) fusion(bf16[2,5120,512]{1,2,0:T(8,128)(2,1)} %get-tuple-element, ...), kind=kLoop, calls=%fused_computation.120.clone.1 | loop fusion | bytes 14680092 | tf_op jit(solution)/shard_map/while/body/eval_jaxpr/dynamic_slice | solution.py:64
  188.6 4.8 %conditional.36 = ((f32[512,8,64]{0,2,1:T(8,128)S(1)}, f32[8,512]{1,0:T(8,128)S(1)})) conditional(s32[]{:T(128)} %bitcast.175, (f32[512,8,64]{0,2,1:T(8,128)S(1)}, f32[8,512]{1,0:T(8,128)S(1)}) %conditional.35, (bf16[2,512,8,64]{1,3,2,0:T(8,128)(2,1)}, bf16[512,8,64]{0,2,1:T(8,128)(2,1)S(1)}, f32[8,512]{1,0:T(8,128)S(1)}, ...), branch_computations={%region_25.25_spmd, %region_26.27_spmd} | conditional | flops 549715968 | bytes 24739892 | solution.py:103
  193.5 4.8 %conditional.38 = ((f32[512,8,64]{0,2,1:T(8,128)S(1)}, f32[8,512]{1,0:T(8,128)S(1)})) conditional(s32[]{:T(128)} %bitcast.173, (f32[512,8,64]{0,2,1:T(8,128)S(1)}, f32[8,512]{1,0:T(8,128)S(1)}) %get-tuple-element.654, (bf16[2,512,8,64]{1,3,2,0:T(8,128)(2,1)}, bf16[512,8,64]{0,2,1:T(8,128)(2,1)S(1)}, f32[8,512]{1,0:T(8,128)S(1)}, ...), branch_computations={%region_31.31_spmd, %region_32.33_spmd} | conditional | flops 549715968 | bytes 24739892 | solution.py:103
  198.3 3.9 %conditional.39 = ((f32[512,8,64]{0,2,1:T(8,128)S(1)}, f32[8,512]{1,0:T(8,128)S(1)})) conditional(s32[]{:T(128)} %bitcast.172, (f32[512,8,64]{0,2,1:T(8,128)S(1)}, f32[8,512]{1,0:T(8,128)S(1)}) %get-tuple-element.655, (bf16[2,512,8,64]{1,3,2,0:T(8,128)(2,1)S(1)}, bf16[512,8,64]{0,2,1:T(8,128)(2,1)S(1)}, f32[8,512]{1,0:T(8,128)S(1)}, ...), branch_computations={%region_34.34_spmd, %region_35.36_spmd} | conditional | flops 549715968 | bytes 20545560 | solution.py:103
  202.2 4.8 %conditional.40 = ((f32[512,8,64]{0,2,1:T(8,128)S(1)}, f32[8,512]{1,0:T(8,128)S(1)})) conditional(s32[]{:T(128)} %bitcast.171, (f32[512,8,64]{0,2,1:T(8,128)S(1)}, f32[8,512]{1,0:T(8,128)S(1)}) %get-tuple-element.656, (bf16[2,512,8,64]{1,3,2,0:T(8,128)(2,1)}, bf16[512,8,64]{0,2,1:T(8,128)(2,1)S(1)}, f32[8,512]{1,0:T(8,128)S(1)}, ...), branch_computations={%region_37.37_spmd, %region_38.39_spmd} | conditional | flops 549715968 | bytes 24739892 | solution.py:103
  207.0 3.9 %conditional.41 = ((f32[512,8,64]{0,2,1:T(8,128)S(1)}, f32[8,512]{1,0:T(8,128)S(1)})) conditional(s32[]{:T(128)} %bitcast.170, (f32[512,8,64]{0,2,1:T(8,128)S(1)}, f32[8,512]{1,0:T(8,128)S(1)}) %get-tuple-element.657, (bf16[2,512,8,64]{1,3,2,0:T(8,128)(2,1)S(1)}, bf16[512,8,64]{0,2,1:T(8,128)(2,1)S(1)}, f32[8,512]{1,0:T(8,128)S(1)}, ...), branch_computations={%region_40.40_spmd, %region_41.42_spmd} | conditional | flops 549715968 | bytes 20545560 | solution.py:103
  213.4 5.5 %constant_dynamic-slice_fusion.10 = (bf16[2,512,512]{1,2,0:T(8,128)(2,1)S(1)}, bf16[2,512,512]{1,2,0:T(8,128)(2,1)}, bf16[2,512,512]{1,2,0:T(8,128)(2,1)}, bf16[...) fusion(bf16[2,5120,512]{1,2,0:T(8,128)(2,1)} %get-tuple-element, ...), kind=kLoop, calls=%fused_computation.120.clone.1 | loop fusion | bytes 14680092 | tf_op jit(solution)/shard_map/while/body/eval_jaxpr/dynamic_slice | solution.py:64
  234.3 3.6 %conditional.35 = (f32[512,8,64]{0,2,1:T(8,128)S(1)}, f32[8,512]{1,0:T(8,128)S(1)}) conditional(s32[]{:T(128)} %bitcast.176, () %tuple.155, (bf16[2,512,8,64]{1,3,2,0:T(8,128)(2,1)S(1)}, bf16[512,8,64]{0,2,1:T(8,128)(2,1)S(1)}, f32[8,512]{1,0:T(8,128)S(1)}) %tuple.229), branch_computations={%region_22.22_spmd, %region_23.24_spmd} | conditional | flops 549449728 | bytes 19447824 | solution.py:103
  237.9 4.8 %conditional.36 = ((f32[512,8,64]{0,2,1:T(8,128)S(1)}, f32[8,512]{1,0:T(8,128)S(1)})) conditional(s32[]{:T(128)} %bitcast.175, (f32[512,8,64]{0,2,1:T(8,128)S(1)}, f32[8,512]{1,0:T(8,128)S(1)}) %conditional.35, (bf16[2,512,8,64]{1,3,2,0:T(8,128)(2,1)}, bf16[512,8,64]{0,2,1:T(8,128)(2,1)S(1)}, f32[8,512]{1,0:T(8,128)S(1)}, ...), branch_computations={%region_25.25_spmd, %region_26.27_spmd} | conditional | flops 549715968 | bytes 24739892 | solution.py:103
  242.8 3.9 %conditional.37 = ((f32[512,8,64]{0,2,1:T(8,128)S(1)}, f32[8,512]{1,0:T(8,128)S(1)})) conditional(s32[]{:T(128)} %bitcast.174, (f32[512,8,64]{0,2,1:T(8,128)S(1)}, f32[8,512]{1,0:T(8,128)S(1)}) %get-tuple-element.653, (bf16[2,512,8,64]{1,3,2,0:T(8,128)(2,1)S(1)}, bf16[512,8,64]{0,2,1:T(8,128)(2,1)S(1)}, f32[8,512]{1,0:T(8,128)S(1)}, ...), branch_computations={%region_28.28_spmd, %region_29.30_spmd} | conditional | flops 549715968 | bytes 20545560 | solution.py:103
  246.6 4.8 %conditional.38 = ((f32[512,8,64]{0,2,1:T(8,128)S(1)}, f32[8,512]{1,0:T(8,128)S(1)})) conditional(s32[]{:T(128)} %bitcast.173, (f32[512,8,64]{0,2,1:T(8,128)S(1)}, f32[8,512]{1,0:T(8,128)S(1)}) %get-tuple-element.654, (bf16[2,512,8,64]{1,3,2,0:T(8,128)(2,1)}, bf16[512,8,64]{0,2,1:T(8,128)(2,1)S(1)}, f32[8,512]{1,0:T(8,128)S(1)}, ...), branch_computations={%region_31.31_spmd, %region_32.33_spmd} | conditional | flops 549715968 | bytes 24739892 | solution.py:103
  253.9 17.9 %all_to_all.70 = bf16[4,256,512]{2,1,0:T(8,128)(2,1)S(1)} all-to-all(bf16[4,256,512]{2,1,0:T(8,128)(2,1)} %bitcast.225), channel_id=1, replica_groups=mesh['grp'=2,'ctx'=4,'head'=2,'rep'=2] {'head','rep'}, dimensions={0} | all-to-all | bytes 2097152 | tf_op jit(solution)/shard_map/all_to_all | solution.py:116
  (134 shorter events, 117.7 us)
Async XLA Ops:
  2.3 17.9 %all-to-all-start = ((bf16[256,4,512]{0,2,1:T(8,128)(2,1)}), bf16[256,4,512]{0,2,1:T(8,128)(2,1)S(1)}, u32[]{:S(2)}, u32[]{:S(2)}) async-start(bf16[256,4,512]{0,2,1:T(8,128)(2,1)} %bitcast.46), calls=%async_computation | async-start | bytes 2097152 | tf_op jit(solution)/shard_map/all_to_all | solution.py:21
  5.8 93.9 %copy-start.7 = (s32[8,8]{1,0:T(8,128)S(1)}, s32[8,8]{1,0:T(8,128)}, u32[]{:S(2)}) copy-start(s32[8,8]{1,0:T(8,128)} %param.38) | copy-start | bytes 772
  5.8 93.9 %copy-start.8 = (s32[8]{0:T(128)S(1)}, s32[8]{0:T(128)}, u32[]{:S(2)}) copy-start(s32[8]{0:T(128)} %param.39) | copy-start | bytes 100
  20.2 17.9 %all-to-all-start.1 = ((bf16[256,4,512]{0,2,1:T(8,128)(2,1)}), bf16[256,4,512]{0,2,1:T(8,128)(2,1)S(1)}, u32[]{:S(2)}, u32[]{:S(2)}) async-start(bf16[256,4,512]{0,2,1:T(8,128)(2,1)} %bitcast.49), calls=%async_computation.1 | async-start | bytes 2097152 | tf_op jit(solution)/shard_map/all_to_all | solution.py:22
  38.9 49.1 %collective-permute-start = (bf16[2,1024,512]{2,1,0:T(8,128)(2,1)S(1)}, bf16[2,1024,512]{2,1,0:T(8,128)(2,1)}, u32[]{:S(2)}, u32[]{:S(2)}) collective-permute-start(bf16[2,1024,512]{2,1,0:T(8,128)(2,1)S(1)} %pad_maximum_fusion), channel_id=1, source_target_pairs={{0,4},{4,8},{8,12},{1,5},{5,9},{9,13},{2,6},{6,10},{10,14},{3,7},{... | collective-permute-start | bytes 6291464 | tf_op jit(solution)/shard_map/ppermute | solution.py:15
  42.3 49.1 %collective-permute-start.2 = (bf16[2,1024,512]{2,1,0:T(8,128)(2,1)S(1)}, bf16[2,1024,512]{2,1,0:T(8,128)(2,1)}, u32[]{:S(2)}, u32[]{:S(2)}) collective-permute-start(bf16[2,1024,512]{2,1,0:T(8,128)(2,1)S(1)} %pad_maximum_fusion), channel_id=1, source_target_pairs={{4,0},{8,4},{12,8},{5,1},{9,5},{13,9},{6,2},{10,6},{14,10},{7,3},{... | collective-permute-start | bytes 6291464 | tf_op jit(solution)/shard_map/ppermute | solution.py:15
  87.9 48.4 %collective-permute-start.1 = (bf16[2,1024,512]{2,1,0:T(8,128)(2,1)}, bf16[2,1024,512]{2,1,0:T(8,128)(2,1)}, u32[]{:S(2)}, u32[]{:S(2)}) collective-permute-start(bf16[2,1024,512]{2,1,0:T(8,128)(2,1)} %collective-permute-done), channel_id=1, source_target_pairs={{0,4},{4,8},{8,12},{1,5},{5,9},{9,13},{2,6},{6,10},{10,14},{3,7},{... | collective-permute-start | bytes 6291464 | tf_op jit(solution)/shard_map/ppermute | solution.py:15
  91.4 55.6 %collective-permute-start.3 = (bf16[2,1024,512]{2,1,0:T(8,128)(2,1)}, bf16[2,1024,512]{2,1,0:T(8,128)(2,1)}, u32[]{:S(2)}, u32[]{:S(2)}) collective-permute-start(bf16[2,1024,512]{2,1,0:T(8,128)(2,1)} %collective-permute-done.2), channel_id=1, source_target_pairs={{4,0},{8,4},{12,8},{5,1},{9,5},{13,9},{6,2},{10,6},{14,10},{7,3},{... | collective-permute-start | bytes 6291464 | tf_op jit(solution)/shard_map/ppermute | solution.py:15
  96.1 17.9 %all-to-all-start.2 = ((bf16[256,4,512]{0,2,1:T(8,128)(2,1)}), bf16[256,4,512]{0,2,1:T(8,128)(2,1)S(1)}, u32[]{:S(2)}, u32[]{:S(2)}) async-start(bf16[256,4,512]{0,2,1:T(8,128)(2,1)} %bitcast.222), calls=%async_computation.2 | async-start | bytes 2097152 | tf_op jit(solution)/shard_map/all_to_all | solution.py:20
  170.7 16.3 %copy-start = (bf16[2,512,512]{1,2,0:T(8,128)(2,1)}, bf16[2,512,512]{1,2,0:T(8,128)(2,1)S(1)}, u32[]{:S(2)}) copy-start(bf16[2,512,512]{1,2,0:T(8,128)(2,1)S(1)} %get-tuple-element.528) | copy-start | bytes 3145732 | tf_op jit(solution)/shard_map/while
  188.6 4.9 %copy-start.5 = (bf16[2,512,512]{1,2,0:T(8,128)(2,1)S(1)}, bf16[2,512,512]{1,2,0:T(8,128)(2,1)}, u32[]{:S(2)}) copy-start(bf16[2,512,512]{1,2,0:T(8,128)(2,1)} %get-tuple-element.524) | copy-start | bytes 3145732 | tf_op jit(solution)/shard_map/while
  188.6 3.0 %copy-start.6 = (bf16[2,512,8,64]{1,3,2,0:T(8,128)(2,1)S(1)}, bf16[2,512,8,64]{1,3,2,0:T(8,128)(2,1)}, u32[]{:S(2)}) copy-start(bf16[2,512,8,64]{1,3,2,0:T(8,128)(2,1)} %get-tuple-element.343) | copy-start | bytes 3145732 | tf_op jit(solution)/shard_map/while/body/eval_jaxpr/cond
  193.5 4.9 %copy-start.3 = (bf16[2,512,512]{1,2,0:T(8,128)(2,1)S(1)}, bf16[2,512,512]{1,2,0:T(8,128)(2,1)}, u32[]{:S(2)}) copy-start(bf16[2,512,512]{1,2,0:T(8,128)(2,1)} %get-tuple-element.526) | copy-start | bytes 3145732 | tf_op jit(solution)/shard_map/while
  193.5 3.0 %copy-start.4 = (bf16[2,512,8,64]{1,3,2,0:T(8,128)(2,1)S(1)}, bf16[2,512,8,64]{1,3,2,0:T(8,128)(2,1)}, u32[]{:S(2)}) copy-start(bf16[2,512,8,64]{1,3,2,0:T(8,128)(2,1)} %get-tuple-element.353) | copy-start | bytes 3145732 | tf_op jit(solution)/shard_map/while/body/eval_jaxpr/cond
  202.2 4.9 %copy-start.1 = (bf16[2,512,512]{1,2,0:T(8,128)(2,1)S(1)}, bf16[2,512,512]{1,2,0:T(8,128)(2,1)}, u32[]{:S(2)}) copy-start(bf16[2,512,512]{1,2,0:T(8,128)(2,1)} %copy-done) | copy-start | bytes 3145732 | tf_op jit(solution)/shard_map/while
  202.2 3.0 %copy-start.2 = (bf16[2,512,8,64]{1,3,2,0:T(8,128)(2,1)S(1)}, bf16[2,512,8,64]{1,3,2,0:T(8,128)(2,1)}, u32[]{:S(2)}) copy-start(bf16[2,512,8,64]{1,3,2,0:T(8,128)(2,1)} %get-tuple-element.363) | copy-start | bytes 3145732 | tf_op jit(solution)/shard_map/while/body/eval_jaxpr/cond
  219.0 15.3 %copy-start = (bf16[2,512,512]{1,2,0:T(8,128)(2,1)}, bf16[2,512,512]{1,2,0:T(8,128)(2,1)S(1)}, u32[]{:S(2)}) copy-start(bf16[2,512,512]{1,2,0:T(8,128)(2,1)S(1)} %get-tuple-element.528) | copy-start | bytes 3145732 | tf_op jit(solution)/shard_map/while
  237.9 4.9 %copy-start.5 = (bf16[2,512,512]{1,2,0:T(8,128)(2,1)S(1)}, bf16[2,512,512]{1,2,0:T(8,128)(2,1)}, u32[]{:S(2)}) copy-start(bf16[2,512,512]{1,2,0:T(8,128)(2,1)} %get-tuple-element.524) | copy-start | bytes 3145732 | tf_op jit(solution)/shard_map/while
  237.9 3.0 %copy-start.6 = (bf16[2,512,8,64]{1,3,2,0:T(8,128)(2,1)S(1)}, bf16[2,512,8,64]{1,3,2,0:T(8,128)(2,1)}, u32[]{:S(2)}) copy-start(bf16[2,512,8,64]{1,3,2,0:T(8,128)(2,1)} %get-tuple-element.343) | copy-start | bytes 3145732 | tf_op jit(solution)/shard_map/while/body/eval_jaxpr/cond
  246.6 4.9 %copy-start.3 = (bf16[2,512,512]{1,2,0:T(8,128)(2,1)S(1)}, bf16[2,512,512]{1,2,0:T(8,128)(2,1)}, u32[]{:S(2)}) copy-start(bf16[2,512,512]{1,2,0:T(8,128)(2,1)} %get-tuple-element.526) | copy-start | bytes 3145732 | tf_op jit(solution)/shard_map/while
  246.7 3.0 %copy-start.4 = (bf16[2,512,8,64]{1,3,2,0:T(8,128)(2,1)S(1)}, bf16[2,512,8,64]{1,3,2,0:T(8,128)(2,1)}, u32[]{:S(2)}) copy-start(bf16[2,512,8,64]{1,3,2,0:T(8,128)(2,1)} %get-tuple-element.353) | copy-start | bytes 3145732 | tf_op jit(solution)/shard_map/while/body/eval_jaxpr/cond
  251.5 1.2 copy-start.1
where the time goes:
time: 275 us; the launch traced here: 274 us
  waiting for transfers between devices  104 us (38%)
  matrix products  58.5 us (21%)
  local copies, waits for them, and re-layouts  57.8 us (21%)
  starting transfers between devices  22.2 us (8%)
  blocking collectives  17.9 us (7%)
  loops' own time  11.2 us (4%)
    ppermute x4, waiting for transfers between devices, from_behind(): return lax.ppermute(x, axis, pairs)  64.2 us
    dot_general x18, matrix products, block_scores(): jnp.einsum('qhd,khd->hqk', query_tile, kv_block[0], preferred_element_typ...  42.2 us
    all_to_all x1, blocking collectives, shards(): lax.all_to_all(attended, ('head', 'rep'), split_axis=0, concat_axis=1, ti...  17.9 us
    unnamed x10, local copies, waits for them, and re-layouts  16 us
    dot_general x9, matrix products, add_weights(): jnp.einsum('hqk,khd->qhd', rounded, value_block, preferred_element_type=j...  15.7 us
    all_to_all x1, waiting for transfers between devices, shards(): lax.all_to_all(values, ('head', 'rep'), split_axis=1, concat_axis=0, tile...  13.8 us
    all_to_all x1, waiting for transfers between devices, shards(): lax.all_to_all(queries, ('head', 'rep'), split_axis=1, concat_axis=0, til...  13.8 us
    while x1, local copies, waits for them, and re-layouts, shards(): tiles_out = lax.map(attend_tile, jnp.arange(tile_count, dtype=jnp.int32))  13.8 us
  transfers between devices with their start and end apart: 7, of which 5 were waited for; matrix products, arithmetic and copies ran while one was open for 6% of the time, Pallas kernels for 0%

commit v1 on v0

--- a/solution.py
+++ b/solution.py
@@ -7,6 +7,18 @@
 HEAD_DIM = 64
 BLOCK = 512
 REACH = 3
+
+
+def exchange_directly(array, axis, split, join):
+    ways, here = (lax.axis_size(axis), lax.axis_index(axis))
+    width = array.shape[split] // ways
+    turned = jnp.roll(array, -here * width, axis=split)
+    got = [lax.slice_in_dim(turned, 0, width, axis=split)]
+    for far in range(1, ways):
+        sent = lax.slice_in_dim(turned, far * width, (far + 1) * width, axis=split)
+        got.append(lax.ppermute(sent, axis, [(d, (d + far) % ways) for d in range(ways)]))
+    line = jnp.concatenate(got[::-1], axis=join)
+    return jnp.roll(line, (here + 1) * got[0].shape[join], axis=join)
 
 
 def from_behind(x, axis, by):
@@ -19,7 +31,7 @@
     query_heads, key_heads, value_heads = (
         lax.all_to_all(queries, ("head", "rep"), split_axis=1, concat_axis=0, tiled=True),
         lax.all_to_all(keys, ("head", "rep"), split_axis=1, concat_axis=0, tiled=True),
-        lax.all_to_all(values, ("head", "rep"), split_axis=1, concat_axis=0, tiled=True),
+        exchange_directly(values, ("head", "rep"), 1, 0),
     )
     row_count, feat_width = query_heads.shape
     heads_dev = feat_width // HEAD_DIM

time: 275 us -> 267 us (0.971)
  waiting for transfers between devices: 104 us -> 96.7 us
    all_to_all x1 -> x0, waiting for transfers between devices: 13.8 us -> none  [shards(): lax.all_to_all(values, ('head', 'rep'), split_axis=1, concat_axis=0, tile...]
    ppermute x0 -> x3, waiting for transfers between devices: none -> 6.91 us  [exchange_directly(): lax.ppermute(sent, axis, [(d, (d + far) % ways) for d in range(ways)])]
    all_to_all x1 -> x0, starting transfers between devices: 3.52 us -> none  [shards(): lax.all_to_all(values, ('head', 'rep'), split_axis=1, concat_axis=0, tile...]
    unnamed x10 -> x16, local copies, waits for them, and re-layouts: 16 us -> 13.9 us
  transfers between devices with their start and end apart: 7 -> 9, of which waited for: 5 -> 6; matrix products, arithmetic and copies ran while one was open for 6% -> 7% of each run, Pallas kernels for 0% -> 0%
where the time goes in v1:
time: 267 us; the launch traced here: 265 us
  waiting for transfers between devices  96.7 us (36%)
  matrix products  58.5 us (22%)
  local copies, waits for them, and re-layouts  56.3 us (21%)
  starting transfers between devices  20.4 us (8%)
  blocking collectives  17.9 us (7%)
  loops' own time  11.3 us (4%)
  other arithmetic  3.69 us (1%)
    ppermute x4, waiting for transfers between devices, from_behind(): return lax.ppermute(x, axis, pairs)  65.1 us
    dot_general x18, matrix products, block_scores(): jnp.einsum('qhd,khd->hqk', query_tile, kv_block[0], preferred_element_typ...  42.2 us
    all_to_all x1, blocking collectives, shards(): lax.all_to_all(attended, ('head', 'rep'), split_axis=0, concat_axis=1, ti...  17.9 us
    dot_general x9, matrix products, add_weights(): jnp.einsum('hqk,khd->qhd', rounded, value_block, preferred_element_type=j...  15.7 us
    unnamed x16, local copies, waits for them, and re-layouts  13.9 us
    while x1, local copies, waits for them, and re-layouts, shards(): tiles_out = lax.map(attend_tile, jnp.arange(tile_count, dtype=jnp.int32))  13.9 us
    all_to_all x1, waiting for transfers between devices, shards(): lax.all_to_all(queries, ('head', 'rep'), split_axis=1, concat_axis=0, til...  13.8 us
    ppermute x4, starting transfers between devices, from_behind(): return lax.ppermute(x, axis, pairs)  11.7 us
  transfers between devices with their start and end apart: 9, of which 6 were waited for; matrix products, arithmetic and copies ran while one was open for 7% of the time, Pallas kernels for 0%

profile of v1, /device:TPU:20, one launch (start us, length us, event | category | flops | bytes accessed | tf_op | source)
XLA Modules:
  0.0 264.9 jit_solution(12173346184395723188)
XLA Ops:
  6.3 3.5 %all-to-all-start = ((bf16[256,4,512]{0,2,1:T(8,128)(2,1)}), bf16[256,4,512]{0,2,1:T(8,128)(2,1)S(1)}, u32[]{:S(2)}, u32[]{:S(2)}) async-start(bf16[256,4,512]{0,2,1:T(8,128)(2,1)} %bitcast.46), calls=%async_computation | async-start | bytes 2097152 | tf_op jit(solution)/shard_map/all_to_all | solution.py:33
  10.3 6.5 %collective-permute-done.1 = bf16[256,512]{1,0:T(8,128)(2,1)S(1)} collective-permute-done((bf16[256,512]{1,0:T(8,128)(2,1)S(1)}, bf16[256,512]{1,0:T(8,128)(2,1)S(1)}, u32[]{:S(2)}, u32[]{:S(2)}) %collective-permute-start.1) | collective-permute-done | bytes 262176 | tf_op jit(solution)/shard_map/ppermute | solution.py:19
  17.1 10.8 %all-to-all-done = bf16[256,4,512]{0,2,1:T(8,128)(2,1)S(1)} async-done(((bf16[256,4,512]{0,2,1:T(8,128)(2,1)}), bf16[256,4,512]{0,2,1:T(8,128)(2,1)S(1)}, u32[]{:S(2)}, u32[]{:S(2)}) %all-to-all-start) | async-done | bytes 1048608 | tf_op jit(solution)/shard_map/all_to_all | solution.py:33
  28.7 3.5 %collective-permute-start.3 = (bf16[2,1024,512]{2,1,0:T(8,128)(2,1)S(1)}, bf16[2,1024,512]{2,1,0:T(8,128)(2,1)}, u32[]{:S(2)}, u32[]{:S(2)}) collective-permute-start(bf16[2,1024,512]{2,1,0:T(8,128)(2,1)S(1)} %pad_maximum_fusion), channel_id=1, source_target_pairs={{0,4},{4,8},{8,12},{1,5},{5,9},{9,13},{2,6},{6,10},{10,14},{3,7},{... | collective-permute-start | bytes 6291464 | tf_op jit(solution)/shard_map/ppermute | solution.py:27
  34.6 43.7 %collective-permute-done.3 = bf16[2,1024,512]{2,1,0:T(8,128)(2,1)} collective-permute-done((bf16[2,1024,512]{2,1,0:T(8,128)(2,1)S(1)}, bf16[2,1024,512]{2,1,0:T(8,128)(2,1)}, u32[]{:S(2)}, u32[]{:S(2)}) %collective-permute-start.3) | collective-permute-done | bytes 2097184 | tf_op jit(solution)/shard_map/ppermute | solution.py:27
  78.2 3.5 %collective-permute-start.4 = (bf16[2,1024,512]{2,1,0:T(8,128)(2,1)}, bf16[2,1024,512]{2,1,0:T(8,128)(2,1)}, u32[]{:S(2)}, u32[]{:S(2)}) collective-permute-start(bf16[2,1024,512]{2,1,0:T(8,128)(2,1)} %collective-permute-done.3), channel_id=1, source_target_pairs={{0,4},{4,8},{8,12},{1,5},{5,9},{9,13},{2,6},{6,10},{10,14},{3,7},{... | collective-permute-start | bytes 6291464 | tf_op jit(solution)/shard_map/ppermute | solution.py:27
  86.4 3.5 %all-to-all-start.1 = ((bf16[256,4,512]{0,2,1:T(8,128)(2,1)}), bf16[256,4,512]{0,2,1:T(8,128)(2,1)S(1)}, u32[]{:S(2)}, u32[]{:S(2)}) async-start(bf16[256,4,512]{0,2,1:T(8,128)(2,1)} %bitcast.218), calls=%async_computation.1 | async-start | bytes 2097152 | tf_op jit(solution)/shard_map/all_to_all | solution.py:32
  90.5 13.8 %all-to-all-done.1 = bf16[256,4,512]{0,2,1:T(8,128)(2,1)S(1)} async-done(((bf16[256,4,512]{0,2,1:T(8,128)(2,1)}), bf16[256,4,512]{0,2,1:T(8,128)(2,1)S(1)}, u32[]{:S(2)}, u32[]{:S(2)}) %all-to-all-start.1) | async-done | bytes 1048608 | tf_op jit(solution)/shard_map/all_to_all | solution.py:32
  105.7 21.5 %collective-permute-done.4 = bf16[2,1024,512]{2,1,0:T(8,128)(2,1)} collective-permute-done((bf16[2,1024,512]{2,1,0:T(8,128)(2,1)}, bf16[2,1024,512]{2,1,0:T(8,128)(2,1)}, u32[]{:S(2)}, u32[]{:S(2)}) %collective-permute-start.4) | collective-permute-done | bytes 2097184 | tf_op jit(solution)/shard_map/ppermute | solution.py:27
  130.2 3.1 %constant_dynamic-update-slice_fusion.10 = bf16[2,5120,512]{2,1,0:T(8,128)(2,1)} fusion(bf16[2,5120,512]{2,1,0:T(8,128)(2,1)} %constant_dynamic-update-slice_fusion.11, bf16[2,1024,512]{2,1,0:T(8,128)(2,1)} %collective-permute-done.3), kind=kLoop, calls=%fused_computation.144 | loop fusion | bytes 4194304
  140.9 13.9 %copy.64 = bf16[2,5120,512]{1,2,0:T(8,128)(2,1)} copy(bf16[2,5120,512]{2,1,0:T(8,128)(2,1)} %constant_dynamic-update-slice_fusion.7) | data formatting | bytes 20971520 | tf_op jit(solution)/shard_map/while | solution.py:126
  154.8 90.3 %while.13 = (s32[]{:T(128)}, bf16[2,512,512]{2,1,0:T(8,128)(2,1)}, s32[2]{0:T(128)S(1)}, s32[]{:T(128)}, f32[14,8]{0,1:T(8,128)S(1)}, /*index=5*/bf16[2,5120,512...) while((s32[]{:T(128)}, bf16[2,512,512]{2,1,0:T(8,128)(2,1)}, ...), condition=%wide.region_43.44_spmd, body=%wide.region_0.43_spmd.sunk | while | flops 5756674048 | bytes 200296880 | solution.py:126
  156.2 5.6 %constant_dynamic-slice_fusion.10 = (bf16[2,512,512]{1,2,0:T(8,128)(2,1)S(1)}, bf16[2,512,512]{1,2,0:T(8,128)(2,1)}, bf16[2,512,512]{1,2,0:T(8,128)(2,1)}, bf16[...) fusion(bf16[2,5120,512]{1,2,0:T(8,128)(2,1)} %get-tuple-element, ...), kind=kLoop, calls=%fused_computation.120.clone.1 | loop fusion | bytes 14680092 | tf_op jit(solution)/shard_map/while/body/eval_jaxpr/dynamic_slice | solution.py:76
  179.6 4.8 %conditional.36 = ((f32[512,8,64]{0,2,1:T(8,128)S(1)}, f32[8,512]{1,0:T(8,128)S(1)})) conditional(s32[]{:T(128)} %bitcast.173, (f32[512,8,64]{0,2,1:T(8,128)S(1)}, f32[8,512]{1,0:T(8,128)S(1)}) %conditional.35, (bf16[2,512,8,64]{1,3,2,0:T(8,128)(2,1)}, bf16[512,8,64]{0,2,1:T(8,128)(2,1)S(1)}, f32[8,512]{1,0:T(8,128)S(1)}, ...), branch_computations={%region_25.25_spmd, %region_26.27_spmd} | conditional | flops 549715968 | bytes 24739892 | solution.py:115
  184.5 4.8 %conditional.38 = ((f32[512,8,64]{0,2,1:T(8,128)S(1)}, f32[8,512]{1,0:T(8,128)S(1)})) conditional(s32[]{:T(128)} %bitcast.171, (f32[512,8,64]{0,2,1:T(8,128)S(1)}, f32[8,512]{1,0:T(8,128)S(1)}) %get-tuple-element.657, (bf16[2,512,8,64]{1,3,2,0:T(8,128)(2,1)}, bf16[512,8,64]{0,2,1:T(8,128)(2,1)S(1)}, f32[8,512]{1,0:T(8,128)S(1)}, ...), branch_computations={%region_31.31_spmd, %region_32.33_spmd} | conditional | flops 549715968 | bytes 24739892 | solution.py:115
  189.3 3.9 %conditional.39 = ((f32[512,8,64]{0,2,1:T(8,128)S(1)}, f32[8,512]{1,0:T(8,128)S(1)})) conditional(s32[]{:T(128)} %bitcast.170, (f32[512,8,64]{0,2,1:T(8,128)S(1)}, f32[8,512]{1,0:T(8,128)S(1)}) %get-tuple-element.658, (bf16[2,512,8,64]{1,3,2,0:T(8,128)(2,1)S(1)}, bf16[512,8,64]{0,2,1:T(8,128)(2,1)S(1)}, f32[8,512]{1,0:T(8,128)S(1)}, ...), branch_computations={%region_34.34_spmd, %region_35.36_spmd} | conditional | flops 549715968 | bytes 20545560 | solution.py:115
  193.2 4.8 %conditional.40 = ((f32[512,8,64]{0,2,1:T(8,128)S(1)}, f32[8,512]{1,0:T(8,128)S(1)})) conditional(s32[]{:T(128)} %bitcast.169, (f32[512,8,64]{0,2,1:T(8,128)S(1)}, f32[8,512]{1,0:T(8,128)S(1)}) %get-tuple-element.659, (bf16[2,512,8,64]{1,3,2,0:T(8,128)(2,1)}, bf16[512,8,64]{0,2,1:T(8,128)(2,1)S(1)}, f32[8,512]{1,0:T(8,128)S(1)}, ...), branch_computations={%region_37.37_spmd, %region_38.39_spmd} | conditional | flops 549715968 | bytes 24739892 | solution.py:115
  198.0 3.9 %conditional.41 = ((f32[512,8,64]{0,2,1:T(8,128)S(1)}, f32[8,512]{1,0:T(8,128)S(1)})) conditional(s32[]{:T(128)} %bitcast.168, (f32[512,8,64]{0,2,1:T(8,128)S(1)}, f32[8,512]{1,0:T(8,128)S(1)}) %get-tuple-element.660, (bf16[2,512,8,64]{1,3,2,0:T(8,128)(2,1)S(1)}, bf16[512,8,64]{0,2,1:T(8,128)(2,1)S(1)}, f32[8,512]{1,0:T(8,128)S(1)}, ...), branch_computations={%region_40.40_spmd, %region_41.42_spmd} | conditional | flops 549715968 | bytes 20545560 | solution.py:115
  204.5 5.6 %constant_dynamic-slice_fusion.10 = (bf16[2,512,512]{1,2,0:T(8,128)(2,1)S(1)}, bf16[2,512,512]{1,2,0:T(8,128)(2,1)}, bf16[2,512,512]{1,2,0:T(8,128)(2,1)}, bf16[...) fusion(bf16[2,5120,512]{1,2,0:T(8,128)(2,1)} %get-tuple-element, ...), kind=kLoop, calls=%fused_computation.120.clone.1 | loop fusion | bytes 14680092 | tf_op jit(solution)/shard_map/while/body/eval_jaxpr/dynamic_slice | solution.py:76
  225.4 3.6 %conditional.35 = (f32[512,8,64]{0,2,1:T(8,128)S(1)}, f32[8,512]{1,0:T(8,128)S(1)}) conditional(s32[]{:T(128)} %bitcast.174, () %tuple.157, (bf16[2,512,8,64]{1,3,2,0:T(8,128)(2,1)S(1)}, bf16[512,8,64]{0,2,1:T(8,128)(2,1)S(1)}, f32[8,512]{1,0:T(8,128)S(1)}) %tuple.231), branch_computations={%region_22.22_spmd, %region_23.24_spmd} | conditional | flops 549449728 | bytes 19447824 | solution.py:115
  229.0 4.8 %conditional.36 = ((f32[512,8,64]{0,2,1:T(8,128)S(1)}, f32[8,512]{1,0:T(8,128)S(1)})) conditional(s32[]{:T(128)} %bitcast.173, (f32[512,8,64]{0,2,1:T(8,128)S(1)}, f32[8,512]{1,0:T(8,128)S(1)}) %conditional.35, (bf16[2,512,8,64]{1,3,2,0:T(8,128)(2,1)}, bf16[512,8,64]{0,2,1:T(8,128)(2,1)S(1)}, f32[8,512]{1,0:T(8,128)S(1)}, ...), branch_computations={%region_25.25_spmd, %region_26.27_spmd} | conditional | flops 549715968 | bytes 24739892 | solution.py:115
  233.9 3.9 %conditional.37 = ((f32[512,8,64]{0,2,1:T(8,128)S(1)}, f32[8,512]{1,0:T(8,128)S(1)})) conditional(s32[]{:T(128)} %bitcast.172, (f32[512,8,64]{0,2,1:T(8,128)S(1)}, f32[8,512]{1,0:T(8,128)S(1)}) %get-tuple-element.656, (bf16[2,512,8,64]{1,3,2,0:T(8,128)(2,1)S(1)}, bf16[512,8,64]{0,2,1:T(8,128)(2,1)S(1)}, f32[8,512]{1,0:T(8,128)S(1)}, ...), branch_computations={%region_28.28_spmd, %region_29.30_spmd} | conditional | flops 549715968 | bytes 20545560 | solution.py:115
  237.8 4.8 %conditional.38 = ((f32[512,8,64]{0,2,1:T(8,128)S(1)}, f32[8,512]{1,0:T(8,128)S(1)})) conditional(s32[]{:T(128)} %bitcast.171, (f32[512,8,64]{0,2,1:T(8,128)S(1)}, f32[8,512]{1,0:T(8,128)S(1)}) %get-tuple-element.657, (bf16[2,512,8,64]{1,3,2,0:T(8,128)(2,1)}, bf16[512,8,64]{0,2,1:T(8,128)(2,1)S(1)}, f32[8,512]{1,0:T(8,128)S(1)}, ...), branch_computations={%region_31.31_spmd, %region_32.33_spmd} | conditional | flops 549715968 | bytes 24739892 | solution.py:115
  245.0 17.9 %all_to_all.54 = bf16[4,256,512]{2,1,0:T(8,128)(2,1)S(1)} all-to-all(bf16[4,256,512]{2,1,0:T(8,128)(2,1)} %bitcast.221), channel_id=1, replica_groups=mesh['grp'=2,'ctx'=4,'head'=2,'rep'=2] {'head','rep'}, dimensions={0} | all-to-all | bytes 2097152 | tf_op jit(solution)/shard_map/all_to_all | solution.py:128
  (147 shorter events, 116.6 us)
Async XLA Ops:
  2.4 7.9 %collective-permute-start = (bf16[256,512]{1,0:T(8,128)(2,1)}, bf16[256,512]{1,0:T(8,128)(2,1)S(1)}, u32[]{:S(2)}, u32[]{:S(2)}) collective-permute-start(bf16[256,512]{1,0:T(8,128)(2,1)} %get-tuple-element.446), channel_id=1, source_target_pairs={{0,3},{1,0},{2,1},{3,2},{4,7},{5,4},{6,5},{7,6},{8,11},{9,8},{10,9... | collective-permute-start | bytes 786440 | tf_op jit(solution)/shard_map/ppermute | solution.py:19
  3.3 13.5 %collective-permute-start.1 = (bf16[256,512]{1,0:T(8,128)(2,1)S(1)}, bf16[256,512]{1,0:T(8,128)(2,1)S(1)}, u32[]{:S(2)}, u32[]{:S(2)}) collective-permute-start(bf16[256,512]{1,0:T(8,128)(2,1)S(1)} %get-tuple-element.445), channel_id=1, source_target_pairs={{0,2},{1,3},{2,0},{3,1},{4,6},{5,7},{6,4},{7,5},{8,10},{9,11},{10,... | collective-permute-start | bytes 786440 | tf_op jit(solution)/shard_map/ppermute | solution.py:19
  3.9 13.0 %collective-permute-start.2 = (bf16[256,512]{1,0:T(8,128)(2,1)S(1)}, bf16[256,512]{1,0:T(8,128)(2,1)S(1)}, u32[]{:S(2)}, u32[]{:S(2)}) collective-permute-start(bf16[256,512]{1,0:T(8,128)(2,1)S(1)} %get-tuple-element.444), channel_id=1, source_target_pairs={{0,1},{1,2},{2,3},{3,0},{4,5},{5,6},{6,7},{7,4},{8,9},{9,10},{10,1... | collective-permute-start | bytes 786440 | tf_op jit(solution)/shard_map/ppermute | solution.py:19
  6.3 21.6 %all-to-all-start = ((bf16[256,4,512]{0,2,1:T(8,128)(2,1)}), bf16[256,4,512]{0,2,1:T(8,128)(2,1)S(1)}, u32[]{:S(2)}, u32[]{:S(2)}) async-start(bf16[256,4,512]{0,2,1:T(8,128)(2,1)} %bitcast.46), calls=%async_computation | async-start | bytes 2097152 | tf_op jit(solution)/shard_map/all_to_all | solution.py:33
  9.9 80.1 %copy-start.7 = (s32[8,8]{1,0:T(8,128)S(1)}, s32[8,8]{1,0:T(8,128)}, u32[]{:S(2)}) copy-start(s32[8,8]{1,0:T(8,128)} %param.38) | copy-start | bytes 772
  9.9 80.1 %copy-start.8 = (s32[8]{0:T(128)S(1)}, s32[8]{0:T(128)}, u32[]{:S(2)}) copy-start(s32[8]{0:T(128)} %param.39) | copy-start | bytes 100
  28.7 49.5 %collective-permute-start.3 = (bf16[2,1024,512]{2,1,0:T(8,128)(2,1)S(1)}, bf16[2,1024,512]{2,1,0:T(8,128)(2,1)}, u32[]{:S(2)}, u32[]{:S(2)}) collective-permute-start(bf16[2,1024,512]{2,1,0:T(8,128)(2,1)S(1)} %pad_maximum_fusion), channel_id=1, source_target_pairs={{0,4},{4,8},{8,12},{1,5},{5,9},{9,13},{2,6},{6,10},{10,14},{3,7},{... | collective-permute-start | bytes 6291464 | tf_op jit(solution)/shard_map/ppermute | solution.py:27
  32.2 49.5 %collective-permute-start.5 = (bf16[2,1024,512]{2,1,0:T(8,128)(2,1)S(1)}, bf16[2,1024,512]{2,1,0:T(8,128)(2,1)}, u32[]{:S(2)}, u32[]{:S(2)}) collective-permute-start(bf16[2,1024,512]{2,1,0:T(8,128)(2,1)S(1)} %pad_maximum_fusion), channel_id=1, source_target_pairs={{4,0},{8,4},{12,8},{5,1},{9,5},{13,9},{6,2},{10,6},{14,10},{7,3},{... | collective-permute-start | bytes 6291464 | tf_op jit(solution)/shard_map/ppermute | solution.py:27
  78.2 48.9 %collective-permute-start.4 = (bf16[2,1024,512]{2,1,0:T(8,128)(2,1)}, bf16[2,1024,512]{2,1,0:T(8,128)(2,1)}, u32[]{:S(2)}, u32[]{:S(2)}) collective-permute-start(bf16[2,1024,512]{2,1,0:T(8,128)(2,1)} %collective-permute-done.3), channel_id=1, source_target_pairs={{0,4},{4,8},{8,12},{1,5},{5,9},{9,13},{2,6},{6,10},{10,14},{3,7},{... | collective-permute-start | bytes 6291464 | tf_op jit(solution)/shard_map/ppermute | solution.py:27
  81.7 56.1 %collective-permute-start.6 = (bf16[2,1024,512]{2,1,0:T(8,128)(2,1)}, bf16[2,1024,512]{2,1,0:T(8,128)(2,1)}, u32[]{:S(2)}, u32[]{:S(2)}) collective-permute-start(bf16[2,1024,512]{2,1,0:T(8,128)(2,1)} %collective-permute-done.5), channel_id=1, source_target_pairs={{4,0},{8,4},{12,8},{5,1},{9,5},{13,9},{6,2},{10,6},{14,10},{7,3},{... | collective-permute-start | bytes 6291464 | tf_op jit(solution)/shard_map/ppermute | solution.py:27
  86.4 17.9 %all-to-all-start.1 = ((bf16[256,4,512]{0,2,1:T(8,128)(2,1)}), bf16[256,4,512]{0,2,1:T(8,128)(2,1)S(1)}, u32[]{:S(2)}, u32[]{:S(2)}) async-start(bf16[256,4,512]{0,2,1:T(8,128)(2,1)} %bitcast.218), calls=%async_computation.1 | async-start | bytes 2097152 | tf_op jit(solution)/shard_map/all_to_all | solution.py:32
  161.7 16.3 %copy-start = (bf16[2,512,512]{1,2,0:T(8,128)(2,1)}, bf16[2,512,512]{1,2,0:T(8,128)(2,1)S(1)}, u32[]{:S(2)}) copy-start(bf16[2,512,512]{1,2,0:T(8,128)(2,1)S(1)} %get-tuple-element.531) | copy-start | bytes 3145732 | tf_op jit(solution)/shard_map/while
  179.6 4.9 %copy-start.5 = (bf16[2,512,512]{1,2,0:T(8,128)(2,1)S(1)}, bf16[2,512,512]{1,2,0:T(8,128)(2,1)}, u32[]{:S(2)}) copy-start(bf16[2,512,512]{1,2,0:T(8,128)(2,1)} %get-tuple-element.527) | copy-start | bytes 3145732 | tf_op jit(solution)/shard_map/while
  179.6 3.0 %copy-start.6 = (bf16[2,512,8,64]{1,3,2,0:T(8,128)(2,1)S(1)}, bf16[2,512,8,64]{1,3,2,0:T(8,128)(2,1)}, u32[]{:S(2)}) copy-start(bf16[2,512,8,64]{1,3,2,0:T(8,128)(2,1)} %get-tuple-element.343) | copy-start | bytes 3145732 | tf_op jit(solution)/shard_map/while/body/eval_jaxpr/cond
  184.5 4.9 %copy-start.3 = (bf16[2,512,512]{1,2,0:T(8,128)(2,1)S(1)}, bf16[2,512,512]{1,2,0:T(8,128)(2,1)}, u32[]{:S(2)}) copy-start(bf16[2,512,512]{1,2,0:T(8,128)(2,1)} %get-tuple-element.529) | copy-start | bytes 3145732 | tf_op jit(solution)/shard_map/while
  184.5 3.0 %copy-start.4 = (bf16[2,512,8,64]{1,3,2,0:T(8,128)(2,1)S(1)}, bf16[2,512,8,64]{1,3,2,0:T(8,128)(2,1)}, u32[]{:S(2)}) copy-start(bf16[2,512,8,64]{1,3,2,0:T(8,128)(2,1)} %get-tuple-element.353) | copy-start | bytes 3145732 | tf_op jit(solution)/shard_map/while/body/eval_jaxpr/cond
  193.2 4.9 %copy-start.1 = (bf16[2,512,512]{1,2,0:T(8,128)(2,1)S(1)}, bf16[2,512,512]{1,2,0:T(8,128)(2,1)}, u32[]{:S(2)}) copy-start(bf16[2,512,512]{1,2,0:T(8,128)(2,1)} %copy-done) | copy-start | bytes 3145732 | tf_op jit(solution)/shard_map/while
  193.2 3.0 %copy-start.2 = (bf16[2,512,8,64]{1,3,2,0:T(8,128)(2,1)S(1)}, bf16[2,512,8,64]{1,3,2,0:T(8,128)(2,1)}, u32[]{:S(2)}) copy-start(bf16[2,512,8,64]{1,3,2,0:T(8,128)(2,1)} %get-tuple-element.363) | copy-start | bytes 3145732 | tf_op jit(solution)/shard_map/while/body/eval_jaxpr/cond
  210.1 15.3 %copy-start = (bf16[2,512,512]{1,2,0:T(8,128)(2,1)}, bf16[2,512,512]{1,2,0:T(8,128)(2,1)S(1)}, u32[]{:S(2)}) copy-start(bf16[2,512,512]{1,2,0:T(8,128)(2,1)S(1)} %get-tuple-element.531) | copy-start | bytes 3145732 | tf_op jit(solution)/shard_map/while
  229.0 4.9 %copy-start.5 = (bf16[2,512,512]{1,2,0:T(8,128)(2,1)S(1)}, bf16[2,512,512]{1,2,0:T(8,128)(2,1)}, u32[]{:S(2)}) copy-start(bf16[2,512,512]{1,2,0:T(8,128)(2,1)} %get-tuple-element.527) | copy-start | bytes 3145732 | tf_op jit(solution)/shard_map/while
  229.0 3.0 %copy-start.6 = (bf16[2,512,8,64]{1,3,2,0:T(8,128)(2,1)S(1)}, bf16[2,512,8,64]{1,3,2,0:T(8,128)(2,1)}, u32[]{:S(2)}) copy-start(bf16[2,512,8,64]{1,3,2,0:T(8,128)(2,1)} %get-tuple-element.343) | copy-start | bytes 3145732 | tf_op jit(solution)/shard_map/while/body/eval_jaxpr/cond
  237.8 4.9 %copy-start.3 = (bf16[2,512,512]{1,2,0:T(8,128)(2,1)S(1)}, bf16[2,512,512]{1,2,0:T(8,128)(2,1)}, u32[]{:S(2)}) copy-start(bf16[2,512,512]{1,2,0:T(8,128)(2,1)} %get-tuple-element.529) | copy-start | bytes 3145732 | tf_op jit(solution)/shard_map/while
  237.8 3.0 %copy-start.4 = (bf16[2,512,8,64]{1,3,2,0:T(8,128)(2,1)S(1)}, bf16[2,512,8,64]{1,3,2,0:T(8,128)(2,1)}, u32[]{:S(2)}) copy-start(bf16[2,512,8,64]{1,3,2,0:T(8,128)(2,1)} %get-tuple-element.353) | copy-start | bytes 3145732 | tf_op jit(solution)/shard_map/while/body/eval_jaxpr/cond
  242.6 1.2 copy-start.1
